TPU v7x, 512 devices: a whole 4x4x16 slice. The times are simulated.
512 devices in a mesh: row: 8 (over z_hi, core), col: 16 (over y, z_lo), depth: 4 (over x).
Axes of the slice: x: 4, y: 4, z: 16 (z_hi: 4, z_lo: 4; z = z_hi * 4 + z_lo), core: 2. Of those that a mesh axis runs over, the one named last changes fastest.
Arguments:
- values: bfloat16 [768, 16, 128, 128], P(('row', 'col')), may hold values from -0.47851562 to 0.47851562
- columns: int32 [768, 16], replicated, may hold values from 0 to 767, as said below
Outputs:
- purified: bfloat16 [768, 16, 128, 128], P(('row', 'col'), 'depth')
Inputs may be any that keep to these rules, and one draw needn't show every extreme that they name: Each block row a names 16 different block columns, a itself among them, all within 8 of a around the cycle of 768 block rows (indices wrap).
All inputs are finite; a program needn't handle non-finite values.
Results may differ from a plain program's by a relative error of at most 0.0047.
Values may be sent and summed in bfloat16 or wider, within the bound.
A program may use at most 128 MiB of HBM per device.

v0:
```python
import jax
import jax.numpy as jnp
from jax import lax
from jax.sharding import PartitionSpec as P

HB = 8


def passed_along(value, axis, by):
    peers = lax.axis_size(axis)
    return lax.ppermute(value, axis, [(i, (i + by) % peers) for i in range(peers)])


def matched_blocks(nearby, band_start, own_cols, target_cols, columns):
    total_blocks = columns.shape[0]
    band_count = nearby.shape[0]
    slot_count = nearby.shape[1]
    partner_cols = jnp.take(columns, own_cols, axis=0)
    same_column = partner_cols[:, :, None, :] == target_cols[:, None, :, None]
    slot_ids = jnp.arange(slot_count, dtype=jnp.int32)
    present = jnp.any(same_column, axis=3)
    chosen = jnp.sum(jnp.where(same_column, slot_ids, 0), axis=3)
    offset = jnp.mod(own_cols - band_start, total_blocks)
    inside = offset < band_count
    usable = inside[:, :, None] & present
    flat_index = jnp.where(
        usable, offset[:, :, None] * slot_count + chosen, band_count * slot_count
    )
    flat_blocks = nearby.reshape(band_count * slot_count, nearby.shape[2], nearby.shape[3])
    return jnp.take(flat_blocks, flat_index, axis=0, mode="fill", fill_value=0)


def local(values, columns):
    own_rows, slot_count, block_size, _ = values.shape
    layers = lax.axis_size("depth")
    quarter = slot_count // layers
    layer_index = lax.axis_index("depth")
    group_index = lax.axis_index(("row", "col"))
    first_row = group_index * own_rows
    own_cols = lax.dynamic_slice_in_dim(columns, first_row, own_rows, 0)
    target_cols = lax.dynamic_slice_in_dim(own_cols, layer_index * quarter, quarter, 1)
    hop_count = (HB + own_rows - 1) // own_rows
    reach_last = HB - (hop_count - 1) * own_rows
    lower_parts = []
    upper_parts = []
    for hop_step in range(1, hop_count + 1):
        edge_rows = own_rows if hop_step < hop_count else reach_last
        from_lower = passed_along(values[own_rows - edge_rows :], ("row", "col"), hop_step)
        from_upper = passed_along(values[:edge_rows], ("row", "col"), -hop_step)
        lower_parts.insert(0, from_lower)
        upper_parts.append(from_upper)
    below_rows = jnp.concatenate(lower_parts, axis=0)
    above_rows = jnp.concatenate(upper_parts, axis=0)
    nearby = jnp.concatenate([below_rows, values, above_rows], axis=0)
    selected = matched_blocks(nearby, first_row - HB, own_cols, target_cols, columns)
    square32 = jnp.einsum("aixy,aijyz->ajxz", values, selected, preferred_element_type=jnp.float32)
    square = square32.astype(jnp.bfloat16)
    whole_square = lax.all_gather(square, "depth", axis=1, tiled=True)
    cube32 = jnp.einsum(
        "aixy,aijyz->ajxz", whole_square, selected, preferred_element_type=jnp.float32
    )
    return (3.0 * square32 - 2.0 * cube32).astype(jnp.bfloat16)


def solution(mesh):
    placed = (P(("row", "col"), None, None, None), P())
    return jax.shard_map(
        local,
        mesh=mesh,
        in_specs=placed,
        out_specs=P(("row", "col"), "depth", None, None),
        check_vma=False,
    )
```

profile of v0, /device:TPU:1, one launch (start us, length us, event | category | flops | bytes accessed | tf_op | source)
XLA Modules:
  0.0 335.9 jit_solution(13076159911926167194)
XLA Ops:
  6.5 4.6 %collective-permute-start.1 = (bf16[6,16,128,128]{3,2,1,0:T(8,128)(2,1)}, bf16[6,16,128,128]{3,2,1,0:T(8,128)(2,1)}, u32[]{:S(2)}, u32[]{:S(2)}) collective-permute-start(bf16[6,16,128,128]{3,2,1,0:T(8,128)(2,1)} %param.2), channel_id=1, source_target_pairs={{0,4},{4,8},{8,12},{12,16},{16,20},{20,24},{24,28},{28,32},{32,36}... | collective-permute-start | bytes 9437192 | tf_op jit(solution)/shard_map/ppermute | solution.py:11
  11.2 7.6 %collective-permute-start.2 = (bf16[6,16,128,128]{3,2,1,0:T(8,128)(2,1)}, bf16[6,16,128,128]{3,2,1,0:T(8,128)(2,1)}, u32[]{:S(2)}, u32[]{:S(2)}) collective-permute-start(bf16[6,16,128,128]{3,2,1,0:T(8,128)(2,1)} %param.2), channel_id=1, source_target_pairs={{0,508},{4,0},{8,4},{12,8},{16,12},{20,16},{24,20},{28,24},{32,28}... | collective-permute-start | bytes 9437192 | tf_op jit(solution)/shard_map/ppermute | solution.py:11
  18.8 3.2 fusion.18
  22.0 1.9 collective-permute-start
  23.9 6.7 %collective-permute-start.3 = (bf16[2,16,128,128]{3,2,1,0:T(8,128)(2,1)}, bf16[2,16,128,128]{3,2,1,0:T(8,128)(2,1)}, u32[]{:S(2)}, u32[]{:S(2)}) collective-permute-start(bf16[2,16,128,128]{3,2,1,0:T(8,128)(2,1)} %get-tuple-element.7), channel_id=1, source_target_pairs={{0,504},{4,508},{8,0},{12,4},{16,8},{20,12},{24,16},{28,20},{32,24... | collective-permute-start | bytes 3145736 | tf_op jit(solution)/shard_map/ppermute | solution.py:11
  30.6 1.0 copy.39
  31.5 0.5 compare_and_fusion.1
  32.1 0.6 reshape.50
  32.7 0.7 pad_clamp_fusion.1
  33.3 1.4 dynamic_slice.7
  34.7 0.8 copy.41
  35.5 1.2 gather_fusion
  36.7 0.9 broadcast_select_fusion.7
  37.6 0.6 compare_reduce_fusion
  38.1 0.6 fusion.14
  38.7 0.1 copy.43
  38.9 0.1 reshape.58
  39.0 0.1 copy.42
  39.1 138.4 %collective-permute-done = bf16[2,16,128,128]{3,2,1,0:T(8,128)(2,1)} collective-permute-done((bf16[2,16,128,128]{3,2,1,0:T(8,128)(2,1)}, bf16[2,16,128,128]{3,2,1,0:T(8,128)(2,1)}, u32[]{:S(2)}, u32[]{:S(2)}) %collective-permute-start) | collective-permute-done | bytes 1048608 | tf_op jit(solution)/shard_map/ppermute | solution.py:11
  177.5 2.4 constant_dynamic-update-slice_fusion.4
  179.8 3.9 %constant_dynamic-update-slice_fusion.3 = bf16[22,16,128,128]{3,2,1,0:T(8,128)(2,1)} fusion(bf16[22,16,128,128]{3,2,1,0:T(8,128)(2,1)} %constant_dynamic-update-slice_fusion.4, bf16[6,16,128,128]{3,2,1,0:T(8,128)(2,1)} %collective-permute-done.1), kind=kLoop, calls=%fused_computation.30 | loop fusion | bytes 6291456
  183.8 2.1 constant_dynamic-update-slice_fusion.2
  185.9 4.0 %constant_dynamic-update-slice_fusion.1 = bf16[22,16,128,128]{3,2,1,0:T(8,128)(2,1)} fusion(bf16[22,16,128,128]{3,2,1,0:T(8,128)(2,1)} %constant_dynamic-update-slice_fusion.2, bf16[6,16,128,128]{3,2,1,0:T(8,128)(2,1)} %collective-permute-done.2), kind=kLoop, calls=%fused_computation.28 | loop fusion | bytes 6291456
  189.8 50.2 %collective-permute-done.3 = bf16[2,16,128,128]{3,2,1,0:T(8,128)(2,1)} collective-permute-done((bf16[2,16,128,128]{3,2,1,0:T(8,128)(2,1)}, bf16[2,16,128,128]{3,2,1,0:T(8,128)(2,1)}, u32[]{:S(2)}, u32[]{:S(2)}) %collective-permute-start.3) | collective-permute-done | bytes 1048608 | tf_op jit(solution)/shard_map/ppermute | solution.py:11
  240.1 2.3 constant_dynamic-update-slice_fusion
  242.4 15.5 %gather_fusion.1 = bf16[384,128,128]{2,1,0:T(8,128)(2,1)} fusion(bf16[352,128,128]{2,1,0:T(8,128)(2,1)} %bitcast.1, s32[1024]{0:T(1024)S(1)} %pad_clamp_fusion), kind=kCustom, calls=%fused_computation.1 | custom fusion | bytes 25167360 | tf_op jit(solution)/shard_map/jit(_take)/gather | solution.py:30
  257.9 7.9 %fusion = f32[6,4,128,128,1]{3,2,1,4,0:T(8,128)S(1)} fusion(bf16[6,16,4,128,128]{4,3,2,1,0:T(8,128)(2,1)} %bitcast.62, pred[6,16,4]{2,1,0:T(8,128)(4,1)S(1)} %copy.42, bf16[6,16,128,128]{3,2,1,0:T(8,128)(2,1)S(1)} %copy-done), kind=kOutput, calls=%fused_computation.3 | convolution fusion | flops 1616904192 | bytes 17301888 | tf_op jit(solution)/shard_map/aixy,aijyz->ajxz/dot_general | solution.py:56
  265.8 1.1 copy-done.1
  266.9 1.0 fusion.13
  268.0 51.1 %all-gather.2.cloned.1.call-done = bf16[6,16,128,128]{2,3,1,0:T(8,128)(2,1)} async-done(((bf16[6,4,128,128]{2,3,1,0:T(8,128)(2,1)}), bf16[6,16,128,128]{2,3,1,0:T(8,128)(2,1)}) %all-gather.2.cloned.1.call-update) | async-done | bytes 3145744 | tf_op jit(solution)/shard_map/all_gather | solution.py:58
  319.1 8.7 %fusion.10 = bf16[6,4,128,128]{2,3,1,0:T(8,128)(2,1)S(1)} fusion(bf16[6,16,128,128]{2,3,1,0:T(8,128)(2,1)} %all-gather.2.cloned.1.call-done, bf16[6,16,4,128,128]{4,3,2,1,0:T(8,128)(2,1)} %bitcast.63, pred[6,16,4]{2,1,0:T(8,128)(4,1)S(1)} %copy.42, f32[6,4,128,128,1]{3,2,1,4,0:T(8,128)} %copy-done.1), kind=kOutput, calls=%fused_computation.14 | convolution fusion | flops 1618477056 | bytes 18088320 | tf_op jit(solution)/shard_map/aixy,aijyz->ajxz/dot_general | solution.py:59
  327.9 1.2 copy.47
  (11 shorter events, 0.1 us)
Async XLA Ops:
  6.5 177.3 %copy-start = (bf16[6,16,128,128]{3,2,1,0:T(8,128)(2,1)S(1)}, bf16[6,16,128,128]{3,2,1,0:T(8,128)(2,1)}, u32[]{:S(2)}) copy-start(bf16[6,16,128,128]{3,2,1,0:T(8,128)(2,1)} %param.2) | copy-start | bytes 9437188
  6.5 312.6 %all-gather.2.cloned.1.call-start = ((), (), s32[]{:S(2)}) async-start(), calls=%async_computation | async-start | bytes 3932160 | tf_op jit(solution)/shard_map/all_gather | solution.py:58
  6.5 173.3 %collective-permute-start.1 = (bf16[6,16,128,128]{3,2,1,0:T(8,128)(2,1)}, bf16[6,16,128,128]{3,2,1,0:T(8,128)(2,1)}, u32[]{:S(2)}, u32[]{:S(2)}) collective-permute-start(bf16[6,16,128,128]{3,2,1,0:T(8,128)(2,1)} %param.2), channel_id=1, source_target_pairs={{0,4},{4,8},{8,12},{12,16},{16,20},{20,24},{24,28},{28,32},{32,36}... | collective-permute-start | bytes 9437192 | tf_op jit(solution)/shard_map/ppermute | solution.py:11
  11.2 174.7 %collective-permute-start.2 = (bf16[6,16,128,128]{3,2,1,0:T(8,128)(2,1)}, bf16[6,16,128,128]{3,2,1,0:T(8,128)(2,1)}, u32[]{:S(2)}, u32[]{:S(2)}) collective-permute-start(bf16[6,16,128,128]{3,2,1,0:T(8,128)(2,1)} %param.2), channel_id=1, source_target_pairs={{0,508},{4,0},{8,4},{12,8},{16,12},{20,16},{24,20},{28,24},{32,28}... | collective-permute-start | bytes 9437192 | tf_op jit(solution)/shard_map/ppermute | solution.py:11
  22.0 155.5 %collective-permute-start = (bf16[2,16,128,128]{3,2,1,0:T(8,128)(2,1)}, bf16[2,16,128,128]{3,2,1,0:T(8,128)(2,1)}, u32[]{:S(2)}, u32[]{:S(2)}) collective-permute-start(bf16[2,16,128,128]{3,2,1,0:T(8,128)(2,1)} %get-tuple-element.8), channel_id=1, source_target_pairs={{0,8},{4,12},{8,16},{12,20},{16,24},{20,28},{24,32},{28,36},{32,40... | collective-permute-start | bytes 3145736 | tf_op jit(solution)/shard_map/ppermute | solution.py:11
  23.9 216.2 %collective-permute-start.3 = (bf16[2,16,128,128]{3,2,1,0:T(8,128)(2,1)}, bf16[2,16,128,128]{3,2,1,0:T(8,128)(2,1)}, u32[]{:S(2)}, u32[]{:S(2)}) collective-permute-start(bf16[2,16,128,128]{3,2,1,0:T(8,128)(2,1)} %get-tuple-element.7), channel_id=1, source_target_pairs={{0,504},{4,508},{8,0},{12,4},{16,8},{20,12},{24,16},{28,20},{32,24... | collective-permute-start | bytes 3145736 | tf_op jit(solution)/shard_map/ppermute | solution.py:11
  265.8 1.1 copy-start.1
Sparse Core Ops, SparseCore 0:
  268.1 50.9 all-gather.1
where the time goes:
time: 336 us
  waiting for transfers between devices  240 us (71%)
  local copies, waits for them, and re-layouts  40.9 us (12%)
  starting transfers between devices  20.8 us (6%)
  matrix products  16.6 us (5%)
  between operations  13.5 us (4%)
  other arithmetic  4.28 us (1%)
    ppermute x4, waiting for transfers between devices, passed_along(): lax.ppermute(value, axis, [(i, (i + by) % peers) for i in range(peers)])  189 us
    all_gather x1, waiting for transfers between devices, local(): whole_square = lax.all_gather(square, 'depth', axis=1, tiled=True)  51.1 us
    ppermute x4, starting transfers between devices, passed_along(): lax.ppermute(value, axis, [(i, (i + by) % peers) for i in range(peers)])  20.8 us
    gather x1, local copies, waits for them, and re-layouts, matched_blocks(): return jnp.take(flat_blocks, flat_index, axis=0, mode='fill', fill_value=0)  15.5 us
    unnamed x9, local copies, waits for them, and re-layouts  14.4 us
    dot_general x1, matrix products, local(): jnp.einsum('aixy,aijyz->ajxz', whole_square, selected, preferred_element_...  8.72 us
    dot_general x1, matrix products, local(): jnp.einsum('aixy,aijyz->ajxz', values, selected, preferred_element_type=j...  7.87 us
  transfers between devices with their start and end apart: 5, of which 3 were waited for; matrix products, arithmetic and copies ran while one was open for 7% of the time, Pallas kernels for 0%

commit v1 on v0

--- a/solution.py
+++ b/solution.py
@@ -4,6 +4,22 @@
 from jax.sharding import PartitionSpec as P
 
 HB = 8
+
+
+def ring_gather(x, axis, dim):
+    ways, here, turn = (lax.axis_size(axis), lax.axis_index(axis), x.shape[dim])
+    shape = [n * ways if d == dim else n for d, n in enumerate(x.shape)]
+    full = lax.dynamic_update_slice_in_dim(jnp.zeros(shape, x.dtype), x, here * turn, axis=dim)
+    going_up = going_down = x
+    for far in range(1, ways // 2 + 1):
+        going_up = lax.ppermute(going_up, axis, [(d, (d + 1) % ways) for d in range(ways)])
+        full = lax.dynamic_update_slice_in_dim(full, going_up, (here - far) % ways * turn, axis=dim)
+        if 2 * far < ways:
+            going_down = lax.ppermute(going_down, axis, [(d, (d - 1) % ways) for d in range(ways)])
+            full = lax.dynamic_update_slice_in_dim(
+                full, going_down, (here + far) % ways * turn, axis=dim
+            )
+    return full
 
 
 def passed_along(value, axis, by):
@@ -55,7 +71,7 @@
     selected = matched_blocks(nearby, first_row - HB, own_cols, target_cols, columns)
     square32 = jnp.einsum("aixy,aijyz->ajxz", values, selected, preferred_element_type=jnp.float32)
     square = square32.astype(jnp.bfloat16)
-    whole_square = lax.all_gather(square, "depth", axis=1, tiled=True)
+    whole_square = ring_gather(square, "depth", 1)
     cube32 = jnp.einsum(
         "aixy,aijyz->ajxz", whole_square, selected, preferred_element_type=jnp.float32
     )

time: 336 us -> 316 us (0.940)
  waiting for transfers between devices: 240 us -> 223 us
  between operations: 13.5 us -> 0.28 us
  starting transfers between devices: 20.8 us -> 29.3 us
  local copies, waits for them, and re-layouts: 40.9 us -> 44.5 us
    all_gather x1 -> x0, waiting for transfers between devices: 51.1 us -> none  [local(): whole_square = lax.all_gather(square, 'depth', axis=1, tiled=True)]
    ppermute x0 -> x3, waiting for transfers between devices: none -> 26.5 us  [the longest x2 26.5 us: ring_gather(): lax.ppermute(going_up, axis, [(d, (d + 1) % ways) for d in range(ways)])]
    ppermute x0 -> x3, starting transfers between devices: none -> 8.59 us  [the longest x2 5.15 us: ring_gather(): lax.ppermute(going_up, axis, [(d, (d + 1) % ways) for d in range(ways)])]
    ppermute x4, waiting for transfers between devices: 189 us -> 196 us  [passed_along(): lax.ppermute(value, axis, [(i, (i + by) % peers) for i in range(peers)])]
    dynamic_update_slice x0 -> x4, local copies, waits for them, and re-layouts: none -> 4.14 us  [the longest x2 2.08 us: ring_gather(): lax.dynamic_update_slice_in_dim(full, going_up, (here - far) % ways * tur...]
    ppermute x0 -> x3, local copies, waits for them, and re-layouts: none -> 3.39 us  [the longest x2 3.01 us: ring_gather(): lax.ppermute(going_up, axis, [(d, (d + 1) % ways) for d in range(ways)])]
    unnamed x9 -> x13, local copies, waits for them, and re-layouts: 14.4 us -> 11.2 us
  transfers between devices with their start and end apart: 5 -> 7, of which waited for: 3 -> 4; matrix products, arithmetic and copies ran while one was open for 7% -> 8% of each run, Pallas kernels for 0% -> 0%
where the time goes in v1:
time: 316 us; the launch traced here: 314 us
  waiting for transfers between devices  223 us (71%)
  local copies, waits for them, and re-layouts  44.5 us (14%)
  starting transfers between devices  29.3 us (9%)
  matrix products  16.3 us (5%)
    ppermute x4, waiting for transfers between devices, passed_along(): lax.ppermute(value, axis, [(i, (i + by) % peers) for i in range(peers)])  196 us
    ppermute x2, waiting for transfers between devices, ring_gather(): lax.ppermute(going_up, axis, [(d, (d + 1) % ways) for d in range(ways)])  26.5 us
    ppermute x4, starting transfers between devices, passed_along(): lax.ppermute(value, axis, [(i, (i + by) % peers) for i in range(peers)])  20.7 us
    gather x1, local copies, waits for them, and re-layouts, matched_blocks(): return jnp.take(flat_blocks, flat_index, axis=0, mode='fill', fill_value=0)  15.5 us
    unnamed x13, local copies, waits for them, and re-layouts  11.2 us
    dot_general x1, matrix products, local(): jnp.einsum('aixy,aijyz->ajxz', whole_square, selected, preferred_element_...  8.47 us
    dot_general x1, matrix products, local(): jnp.einsum('aixy,aijyz->ajxz', values, selected, preferred_element_type=j...  7.87 us
  transfers between devices with their start and end apart: 7, of which 4 were waited for; matrix products, arithmetic and copies ran while one was open for 8% of the time, Pallas kernels for 0%

profile of v1, /device:TPU:1, one launch (start us, length us, event | category | flops | bytes accessed | tf_op | source)
XLA Modules:
  0.0 314.4 jit_solution(13982250647826874787)
XLA Ops:
  0.0 4.5 %collective-permute-start.1 = (bf16[6,16,128,128]{3,2,1,0:T(8,128)(2,1)}, bf16[6,16,128,128]{3,2,1,0:T(8,128)(2,1)}, u32[]{:S(2)}, u32[]{:S(2)}) collective-permute-start(bf16[6,16,128,128]{3,2,1,0:T(8,128)(2,1)} %param.2), channel_id=1, source_target_pairs={{0,4},{4,8},{8,12},{12,16},{16,20},{20,24},{24,28},{28,32},{32,36}... | collective-permute-start | bytes 9437192 | tf_op jit(solution)/shard_map/ppermute | solution.py:27
  4.5 7.6 %collective-permute-start.2 = (bf16[6,16,128,128]{3,2,1,0:T(8,128)(2,1)}, bf16[6,16,128,128]{3,2,1,0:T(8,128)(2,1)}, u32[]{:S(2)}, u32[]{:S(2)}) collective-permute-start(bf16[6,16,128,128]{3,2,1,0:T(8,128)(2,1)} %param.2), channel_id=1, source_target_pairs={{0,508},{4,0},{8,4},{12,8},{16,12},{20,16},{24,20},{28,24},{32,28}... | collective-permute-start | bytes 9437192 | tf_op jit(solution)/shard_map/ppermute | solution.py:27
  12.2 2.7 fusion.18
  14.9 1.9 collective-permute-start
  16.8 6.7 %collective-permute-start.3 = (bf16[2,16,128,128]{3,2,1,0:T(8,128)(2,1)}, bf16[2,16,128,128]{3,2,1,0:T(8,128)(2,1)}, u32[]{:S(2)}, u32[]{:S(2)}) collective-permute-start(bf16[2,16,128,128]{3,2,1,0:T(8,128)(2,1)} %get-tuple-element.7), channel_id=1, source_target_pairs={{0,504},{4,508},{8,0},{12,4},{16,8},{20,12},{24,16},{28,20},{32,24... | collective-permute-start | bytes 3145736 | tf_op jit(solution)/shard_map/ppermute | solution.py:27
  23.8 0.6 gather_fusion
  24.7 0.6 compare_reduce_fusion
  25.3 0.6 fusion.14
  26.2 144.5 %collective-permute-done = bf16[2,16,128,128]{3,2,1,0:T(8,128)(2,1)S(1)} collective-permute-done((bf16[2,16,128,128]{3,2,1,0:T(8,128)(2,1)S(1)}, bf16[2,16,128,128]{3,2,1,0:T(8,128)(2,1)S(1)}, u32[]{:S(2)}, u32[]{:S(2)}) %collective-permute-start) | collective-permute-done | bytes 1048608 | tf_op jit(solution)/shard_map/ppermute | solution.py:27
  170.7 1.1 constant_dynamic-update-slice_fusion.4
  171.8 4.1 %constant_dynamic-update-slice_fusion.3 = bf16[22,16,128,128]{3,2,1,0:T(8,128)(2,1)} fusion(bf16[22,16,128,128]{3,2,1,0:T(8,128)(2,1)} %constant_dynamic-update-slice_fusion.4, bf16[6,16,128,128]{3,2,1,0:T(8,128)(2,1)} %collective-permute-done.1), kind=kLoop, calls=%fused_computation.30 | loop fusion | bytes 6291456
  175.9 1.9 constant_dynamic-update-slice_fusion.2
  177.8 4.0 %constant_dynamic-update-slice_fusion.1 = bf16[22,16,128,128]{3,2,1,0:T(8,128)(2,1)} fusion(bf16[22,16,128,128]{3,2,1,0:T(8,128)(2,1)} %constant_dynamic-update-slice_fusion.2, bf16[6,16,128,128]{3,2,1,0:T(8,128)(2,1)} %collective-permute-done.2), kind=kLoop, calls=%fused_computation.28 | loop fusion | bytes 6291456
  181.8 51.7 %collective-permute-done.3 = bf16[2,16,128,128]{3,2,1,0:T(8,128)(2,1)} collective-permute-done((bf16[2,16,128,128]{3,2,1,0:T(8,128)(2,1)}, bf16[2,16,128,128]{3,2,1,0:T(8,128)(2,1)}, u32[]{:S(2)}, u32[]{:S(2)}) %collective-permute-start.3) | collective-permute-done | bytes 1048608 | tf_op jit(solution)/shard_map/ppermute | solution.py:27
  233.4 2.3 constant_dynamic-update-slice_fusion
  235.7 15.5 %gather_fusion.1 = bf16[384,128,128]{2,1,0:T(8,128)(2,1)} fusion(bf16[352,128,128]{2,1,0:T(8,128)(2,1)} %bitcast.1, s32[1024]{0:T(1024)S(1)} %pad_clamp_fusion), kind=kCustom, calls=%fused_computation.1 | custom fusion | bytes 25167360 | tf_op jit(solution)/shard_map/jit(_take)/gather | solution.py:46
  251.3 7.9 %fusion = f32[6,4,128,128,1]{3,2,1,4,0:T(8,128)S(1)} fusion(bf16[6,16,4,128,128]{4,3,2,1,0:T(8,128)(2,1)} %bitcast.62, pred[6,16,4]{2,1,0:T(8,128)(4,1)S(1)} %copy.51, bf16[6,16,128,128]{3,2,1,0:T(8,128)(2,1)S(1)} %copy-done), kind=kOutput, calls=%fused_computation.3 | convolution fusion | flops 1616904192 | bytes 17301888 | tf_op jit(solution)/shard_map/aixy,aijyz->ajxz/dot_general | solution.py:72
  259.3 3.1 collective-permute-start.4
  262.4 3.4 %collective-permute-start.5 = (bf16[6,4,128,128]{2,3,1,0:T(8,128)(2,1)S(1)}, bf16[6,4,128,128]{2,3,1,0:T(8,128)(2,1)S(1)}, u32[]{:S(2)}, u32[]{:S(2)}) collective-permute-start(bf16[6,4,128,128]{2,3,1,0:T(8,128)(2,1)S(1)} %fusion.13), channel_id=1, source_target_pairs={{0,3},{1,0},{2,1},{3,2},{4,7},{5,4},{6,5},{7,6},{8,11},{9,8},{10,9... | collective-permute-start | bytes 2359304 | tf_op jit(solution)/shard_map/ppermute | solution.py:18
  265.8 15.3 %collective-permute-done.4 = bf16[6,4,128,128]{2,3,1,0:T(8,128)(2,1)} collective-permute-done((bf16[6,4,128,128]{2,3,1,0:T(8,128)(2,1)S(1)}, bf16[6,4,128,128]{2,3,1,0:T(8,128)(2,1)}, u32[]{:S(2)}, u32[]{:S(2)}) %collective-permute-start.4) | collective-permute-done | bytes 786464 | tf_op jit(solution)/shard_map/ppermute | solution.py:15
  281.1 2.1 collective-permute-start.6
  283.3 0.4 copy.54
  283.7 2.4 broadcast_in_dim.52
  286.1 1.0 constant_dynamic-update-slice_fusion.7
  287.1 1.5 copy.55
  289.1 1.0 constant_dynamic-update-slice_fusion.6
  290.1 1.0 constant_dynamic-update-slice_fusion.5
  291.1 11.1 %collective-permute-done.6 = bf16[6,4,128,128]{2,3,1,0:T(8,128)(2,1)} collective-permute-done((bf16[6,4,128,128]{2,3,1,0:T(8,128)(2,1)}, bf16[6,4,128,128]{2,3,1,0:T(8,128)(2,1)}, u32[]{:S(2)}, u32[]{:S(2)}) %collective-permute-start.6) | collective-permute-done | bytes 786464 | tf_op jit(solution)/shard_map/ppermute | solution.py:15
  302.2 1.5 copy.57
  303.7 1.1 constant_dynamic-update-slice_fusion.8
  304.8 8.5 %fusion.10 = bf16[6,4,128,128]{2,3,1,0:T(8,128)(2,1)S(1)} fusion(bf16[6,16,128,128]{3,2,1,0:T(8,128)(2,1)} %constant_dynamic-update-slice_fusion.8, bf16[6,16,4,128,128]{4,3,2,1,0:T(8,128)(2,1)} %bitcast.63, pred[6,16,4]{2,1,0:T(8,128)(4,1)S(1)} %copy.51, f32[6,4,128,128,1]{3,2,1,4,0:T(8,128)S(1)} %copy-done.2), kind=kOutput, calls=%fused_computation.14 | convolution fusion | flops 1618477056 | bytes 18088320 | tf_op jit(solution)/shard_map/aixy,aijyz->ajxz/dot_general | solution.py:75
  313.3 1.2 copy.59
  (27 shorter events, 1.5 us)
Async XLA Ops:
  0.0 23.5 %copy-start.3 = (s32[768,16]{0,1:T(8,128)S(1)}, s32[768,16]{0,1:T(8,128)}, u32[]{:S(2)}) copy-start(s32[768,16]{0,1:T(8,128)} %param.3) | copy-start | bytes 147460
  0.0 171.8 %collective-permute-start.1 = (bf16[6,16,128,128]{3,2,1,0:T(8,128)(2,1)}, bf16[6,16,128,128]{3,2,1,0:T(8,128)(2,1)}, u32[]{:S(2)}, u32[]{:S(2)}) collective-permute-start(bf16[6,16,128,128]{3,2,1,0:T(8,128)(2,1)} %param.2), channel_id=1, source_target_pairs={{0,4},{4,8},{8,12},{12,16},{16,20},{20,24},{24,28},{28,32},{32,36}... | collective-permute-start | bytes 9437192 | tf_op jit(solution)/shard_map/ppermute | solution.py:27
  4.5 173.3 %collective-permute-start.2 = (bf16[6,16,128,128]{3,2,1,0:T(8,128)(2,1)}, bf16[6,16,128,128]{3,2,1,0:T(8,128)(2,1)}, u32[]{:S(2)}, u32[]{:S(2)}) collective-permute-start(bf16[6,16,128,128]{3,2,1,0:T(8,128)(2,1)} %param.2), channel_id=1, source_target_pairs={{0,508},{4,0},{8,4},{12,8},{16,12},{20,16},{24,20},{28,24},{32,28}... | collective-permute-start | bytes 9437192 | tf_op jit(solution)/shard_map/ppermute | solution.py:27
  14.9 155.8 %collective-permute-start = (bf16[2,16,128,128]{3,2,1,0:T(8,128)(2,1)S(1)}, bf16[2,16,128,128]{3,2,1,0:T(8,128)(2,1)S(1)}, u32[]{:S(2)}, u32[]{:S(2)}) collective-permute-start(bf16[2,16,128,128]{3,2,1,0:T(8,128)(2,1)S(1)} %get-tuple-element.8), channel_id=1, source_target_pairs={{0,8},{4,12},{8,16},{12,20},{16,24},{20,28},{24,32},{28,36},{32,40... | collective-permute-start | bytes 3145736 | tf_op jit(solution)/shard_map/ppermute | solution.py:27
  16.8 216.6 %collective-permute-start.3 = (bf16[2,16,128,128]{3,2,1,0:T(8,128)(2,1)}, bf16[2,16,128,128]{3,2,1,0:T(8,128)(2,1)}, u32[]{:S(2)}, u32[]{:S(2)}) collective-permute-start(bf16[2,16,128,128]{3,2,1,0:T(8,128)(2,1)} %get-tuple-element.7), channel_id=1, source_target_pairs={{0,504},{4,508},{8,0},{12,4},{16,8},{20,12},{24,16},{28,20},{32,24... | collective-permute-start | bytes 3145736 | tf_op jit(solution)/shard_map/ppermute | solution.py:27
  171.8 4.1 %copy-start = (bf16[6,16,128,128]{3,2,1,0:T(8,128)(2,1)S(1)}, bf16[6,16,128,128]{3,2,1,0:T(8,128)(2,1)}, u32[]{:S(2)}) copy-start(bf16[6,16,128,128]{3,2,1,0:T(8,128)(2,1)} %param.2) | copy-start | bytes 9437188
  259.1 22.0 %copy-start.1 = (f32[6,4,128,128,1]{3,2,1,4,0:T(8,128)}, f32[6,4,128,128,1]{3,2,1,4,0:T(8,128)S(1)}, u32[]{:S(2)}) copy-start(f32[6,4,128,128,1]{3,2,1,4,0:T(8,128)S(1)} %fusion) | copy-start | bytes 4718596
  259.3 21.8 %collective-permute-start.4 = (bf16[6,4,128,128]{2,3,1,0:T(8,128)(2,1)S(1)}, bf16[6,4,128,128]{2,3,1,0:T(8,128)(2,1)}, u32[]{:S(2)}, u32[]{:S(2)}) collective-permute-start(bf16[6,4,128,128]{2,3,1,0:T(8,128)(2,1)S(1)} %fusion.13), channel_id=1, source_target_pairs={{0,1},{1,2},{2,3},{3,0},{4,5},{5,6},{6,7},{7,4},{8,9},{9,10},{10,1... | collective-permute-start | bytes 2359304 | tf_op jit(solution)/shard_map/ppermute | solution.py:15
  262.4 26.3 %collective-permute-start.5 = (bf16[6,4,128,128]{2,3,1,0:T(8,128)(2,1)S(1)}, bf16[6,4,128,128]{2,3,1,0:T(8,128)(2,1)S(1)}, u32[]{:S(2)}, u32[]{:S(2)}) collective-permute-start(bf16[6,4,128,128]{2,3,1,0:T(8,128)(2,1)S(1)} %fusion.13), channel_id=1, source_target_pairs={{0,3},{1,0},{2,1},{3,2},{4,7},{5,4},{6,5},{7,6},{8,11},{9,8},{10,9... | collective-permute-start | bytes 2359304 | tf_op jit(solution)/shard_map/ppermute | solution.py:18
  281.1 21.1 %collective-permute-start.6 = (bf16[6,4,128,128]{2,3,1,0:T(8,128)(2,1)}, bf16[6,4,128,128]{2,3,1,0:T(8,128)(2,1)}, u32[]{:S(2)}, u32[]{:S(2)}) collective-permute-start(bf16[6,4,128,128]{2,3,1,0:T(8,128)(2,1)} %collective-permute-done.4), channel_id=1, source_target_pairs={{0,1},{1,2},{2,3},{3,0},{4,5},{5,6},{6,7},{7,4},{8,9},{9,10},{10,1... | collective-permute-start | bytes 2359304 | tf_op jit(solution)/shard_map/ppermute | solution.py:15
  289.1 15.8 %copy-start.2 = (f32[6,4,128,128,1]{3,2,1,4,0:T(8,128)S(1)}, f32[6,4,128,128,1]{3,2,1,4,0:T(8,128)}, u32[]{:S(2)}) copy-start(f32[6,4,128,128,1]{3,2,1,4,0:T(8,128)} %copy-done.1) | copy-start | bytes 4718596
